TPU v7x, 256 devices: a whole 4x4x8 slice. The times are simulated.
256 devices in a mesh: dp: 4 (over y), graph: 64 (over z, x, core).
Axes of the slice: x: 4, y: 4, z: 8, core: 2. Of those that a mesh axis runs over, the one named last changes fastest.
Arguments:
- edge_state: bfloat16 [4, 131072, 512], P('dp', 'graph'), may hold values from -6 to 6
- cotangent: bfloat16 [4, 131072, 512], P('dp', 'graph'), may hold values from -6 to 6
- edge_count: int32 [4, 64], P('dp', 'graph'), may hold values from 1024 to 2048, as said below
- triplet_basis: bfloat16 [4, 16, 524288], P('dp', None, 'graph'), may hold values from -6 to 6
- triplet_in: int32 [4, 524288], P('dp', 'graph'), may hold values from 0 to 2047, as said below
- triplet_out: int32 [4, 524288], P('dp', 'graph'), may hold values from 0 to 2047, as said below
- down_weight: bfloat16 [512, 64], replicated, may hold values from -0.25 to 0.25
- basis_weight: bfloat16 [16, 64], replicated, may hold values from -1.5 to 1.5
- bilinear_weight: bfloat16 [64, 64], replicated, may hold values from -0.75 to 0.75
- up_weight: bfloat16 [64, 512], replicated, may hold values from -0.75 to 0.75
- first_weight: bfloat16 [512, 512], replicated, may hold values from -0.25 to 0.25
- second_weight: bfloat16 [512, 512], replicated, may hold values from -0.25 to 0.25
Outputs:
- edge_grad: bfloat16 [4, 131072, 512], P('dp', 'graph')
- down_grad: float32 [512, 64], replicated
- basis_grad: float32 [16, 64], replicated
- bilinear_grad: float32 [64, 64], replicated
- up_grad: float32 [64, 512], replicated
- first_grad: float32 [512, 512], replicated
- second_grad: float32 [512, 512], replicated
Inputs may be any that keep to these rules, and one draw needn't show every extreme that they name: `edge_count`: every entry is a multiple of 128; in every batch some shard holds all 2048 slots live. Slot s * 8192 + j * 128 + k (s and j below 64, k below 128) holds a triplet of shard s whose in-edge is row triplet_in of shard j, a live row: below edge_count[b, j]. Slot s * 8192 + t holds a triplet whose out-edge is row triplet_out of shard s, a live row: below edge_count[b, s].
All inputs are finite; a program needn't handle non-finite values.
Results may differ from a plain program's by a relative error of at most 0.0096.
Values may be sent and summed in bfloat16 or wider, within the bound.
A program may use at most 128 MiB of HBM per device.

v0:
```python
import math
import jax
import jax.numpy as jnp
from jax import lax
from jax.sharding import PartitionSpec as P

HALF = 0.7071067811865476


def silu_slope(argument):
    logistic = jax.nn.sigmoid(argument)
    return logistic * (1.0 + argument * (1.0 - logistic))


def contract(left, right, left_dim, right_dim):
    return lax.dot_general(
        left, right, (((left_dim,), (right_dim,)), ((), ())), preferred_element_type=jnp.float32
    )


def local(
    edge_state,
    cotangent,
    edge_count,
    triplet_basis,
    triplet_in,
    triplet_out,
    down_weight,
    basis_weight,
    bilinear_weight,
    up_weight,
    first_weight,
    second_weight,
):
    edge_rows = edge_state[0]
    row_count = edge_rows.shape[0]
    shards = lax.axis_size("graph")
    narrow = down_weight.shape[1]
    in_local = triplet_in[0]
    out_local = triplet_out[0]
    tri_rows = in_local.shape[0]
    slot_count = tri_rows // shards
    live_mask = (jnp.arange(row_count, dtype=jnp.int32) < edge_count[0, 0]).astype(jnp.float32)
    wanted = lax.all_to_all(
        in_local.reshape(shards, slot_count), "graph", split_axis=0, concat_axis=0, tiled=True
    ).reshape(tri_rows)
    pre_down = contract(down_weight, edge_rows, 0, 1)
    down_rows = jax.nn.silu(pre_down).astype(jnp.bfloat16)
    tri_coef = contract(basis_weight, triplet_basis[0], 0, 0)
    served = jnp.take(down_rows, wanted, axis=1).reshape(narrow, shards, slot_count)
    fetched = lax.all_to_all(served, "graph", split_axis=1, concat_axis=1, tiled=True).reshape(
        narrow, tri_rows
    )
    message = tri_coef * fetched.astype(jnp.float32)
    gathered = (
        jnp.zeros((narrow, row_count), jnp.float32)
        .at[:, out_local]
        .add(message)
        .astype(jnp.bfloat16)
    )
    mixed_rows = contract(bilinear_weight, gathered, 0, 0).astype(jnp.bfloat16)
    pre_up = contract(mixed_rows, up_weight, 0, 0)
    summed = edge_rows.astype(jnp.float32) + jax.nn.silu(pre_up)
    summed_half = summed.astype(jnp.bfloat16)
    pre_first = jnp.dot(summed_half, first_weight, preferred_element_type=jnp.float32)
    first_rows = jax.nn.silu(pre_first).astype(jnp.bfloat16)
    pre_second = jnp.dot(first_rows, second_weight, preferred_element_type=jnp.float32)
    back_top = cotangent[0].astype(jnp.float32) * live_mask[:, None] * HALF
    back_second = (back_top * silu_slope(pre_second)).astype(jnp.bfloat16)
    back_first = (contract(back_second, second_weight, 1, 1) * silu_slope(pre_first)).astype(
        jnp.bfloat16
    )
    first_grad = contract(summed_half, back_first, 0, 0)
    second_grad = contract(first_rows, back_second, 0, 0)
    back_summed = back_top + contract(back_first, first_weight, 1, 1)
    back_up = (back_summed * silu_slope(pre_up)).astype(jnp.bfloat16)
    back_mixed = contract(up_weight, back_up, 1, 1).astype(jnp.bfloat16)
    back_gathered = contract(bilinear_weight, back_mixed, 1, 0)
    back_message = jnp.take(back_gathered, out_local, axis=1)
    back_coef = (back_message * fetched.astype(jnp.float32)).astype(jnp.bfloat16)
    back_fetched = back_message * tri_coef
    returned = (
        lax.all_to_all(
            back_fetched.reshape(narrow, shards, slot_count).astype(jnp.bfloat16),
            "graph",
            split_axis=1,
            concat_axis=1,
            tiled=True,
        )
        .astype(jnp.float32)
        .reshape(narrow, tri_rows)
    )
    back_down = jnp.zeros((narrow, row_count), jnp.float32).at[:, wanted].add(returned)
    up_grad = contract(mixed_rows, back_up, 1, 0)
    bilinear_grad = contract(gathered, back_mixed, 1, 1)
    basis_grad = contract(triplet_basis[0], back_coef, 1, 1)
    back_pre = (back_down * silu_slope(pre_down)).astype(jnp.bfloat16)
    down_grad = contract(edge_rows, back_pre, 0, 1)
    edge_grad = (back_summed + contract(back_pre, down_weight, 0, 1)).astype(jnp.bfloat16)
    down_grad, basis_grad, bilinear_grad, up_grad, first_grad, second_grad = lax.psum(
        (down_grad, basis_grad, bilinear_grad, up_grad, first_grad, second_grad), ("dp", "graph")
    )
    grad_scale = 1.0 / math.sqrt(lax.axis_size("dp") * shards * row_count)
    return (
        edge_grad[None],
        down_grad * grad_scale,
        basis_grad * grad_scale,
        bilinear_grad * grad_scale,
        up_grad * grad_scale,
        first_grad * grad_scale,
        second_grad * grad_scale,
    )


def solution(mesh):
    in_specs = (
        P("dp", "graph", None),
        P("dp", "graph", None),
        P("dp", "graph"),
        P("dp", None, "graph"),
        P("dp", "graph"),
        P("dp", "graph"),
        P(),
        P(),
        P(),
        P(),
        P(),
        P(),
    )
    out_specs = (P("dp", "graph", None), P(), P(), P(), P(), P(), P())
    return jax.shard_map(local, mesh=mesh, in_specs=in_specs, out_specs=out_specs, check_vma=False)
```

profile of v0, /device:TPU:2, one launch (start us, length us, event | category | flops | bytes accessed | tf_op | source)
XLA Modules:
  0.0 558.6 jit_solution(4663164017009512426)
XLA Ops:
  7.2 0.0 copy-start
  7.2 12.2 %all-to-all-start = ((s32[64,1,128]{2,1,0:T(1,128)}), s32[64,1,128]{2,1,0:T(1,128)S(1)}, u32[]{:S(2)}, u32[]{:S(2)}) async-start(s32[64,1,128]{2,1,0:T(1,128)} %bitcast.127), calls=%async_computation | async-start | bytes 65536 | tf_op jit(solution)/shard_map/all_to_all | solution.py:44
  20.0 0.8 compare_and_fusion.1
  20.8 3.2 multiply_convert_fusion.4
  24.0 0.3 copy.35
  24.3 3.6 all-to-all-done
  28.0 24.0 %gather_fusion = bf16[8192,64]{1,0:T(8,128)(2,1)S(1)} fusion(bf16[64,2048]{0,1:T(8,128)(2,1)S(1)} %copy.35, s32[8192]{0:T(1024)S(1)} %broadcast_clamp_fusion.1), kind=kCustom, calls=%fused_computation | custom fusion | bytes 2129920 | tf_op jit(solution)/shard_map/jit(_take)/gather | solution.py:50
  52.0 1.6 copy.36
  53.6 2.4 broadcast_select_fusion
  56.0 6.9 %all-to-all-start.1 = ((bf16[64,64,128]{2,0,1:T(8,128)(2,1)}), bf16[64,64,128]{2,0,1:T(8,128)(2,1)}, u32[]{:S(2)}, u32[]{:S(2)}) async-start(bf16[64,64,128]{2,0,1:T(8,128)(2,1)} %broadcast_select_fusion), calls=%async_computation.1 | async-start | bytes 2097152 | tf_op jit(solution)/shard_map/all_to_all | solution.py:51
  62.9 0.0 copy-done.8
  62.9 0.0 copy-done.9
  63.0 0.4 fusion.25
  63.4 28.1 %all-to-all-done.1 = bf16[64,64,128]{2,0,1:T(8,128)(2,1)} async-done(((bf16[64,64,128]{2,0,1:T(8,128)(2,1)}), bf16[64,64,128]{2,0,1:T(8,128)(2,1)}, u32[]{:S(2)}, u32[]{:S(2)}) %all-to-all-start.1) | async-done | bytes 1048608 | tf_op jit(solution)/shard_map/all_to_all | solution.py:51
  91.5 2.7 fusion.6
  94.3 3.8 copy.38
  98.1 45.3 %scatter_custom_fusion = f32[64,2048]{0,1:T(8,128)} fusion(s32[8192]{0:T(1024)S(1)} %bitcast.126, f32[8192,64]{1,0:T(8,128)} %copy.38, f32[]{:T(128)} %constant.18.clone.1), kind=kCustom, calls=%fused_computation.50 | custom fusion | flops 524288 | bytes 524800 | tf_op jit(solution)/shard_map/scatter-add | solution.py:58
  143.4 1.5 convolution_convert_fusion.1
  144.9 2.9 add_convert_fusion.1
  147.8 0.0 copy-start.14
  147.9 0.0 copy-start.15
  147.9 1.9 multiply_convert_fusion.2
  149.8 0.4 copy-done.14
  150.2 0.1 copy-done.15
  150.3 2.6 fusion.3
  152.9 2.3 multiply_convert_fusion.1
  155.3 4.0 multiply_convert_fusion
  159.2 0.7 convolution_convert_fusion
  160.0 0.6 copy-done.4
  160.6 0.7 copy-done.6
  161.3 1.0 convolution_bitcast_fusion
  162.3 1.4 copy.39
  163.6 27.9 %gather_fusion.1 = f32[8192,64]{1,0:T(8,128)} fusion(f32[64,2048]{0,1:T(8,128)S(1)} %copy.39, s32[8192]{0:T(1024)S(1)} %broadcast_clamp_fusion), kind=kCustom, calls=%fused_computation.1 | custom fusion | bytes 4227072 | tf_op jit(solution)/shard_map/jit(_take)/gather | solution.py:79
  191.6 3.8 copy.40
  195.3 2.9 copy_bitcast_fusion
  198.2 5.8 %all-to-all-start.2 = ((bf16[64,64,128]{2,0,1:T(8,128)(2,1)}), bf16[64,64,128]{2,0,1:T(8,128)(2,1)S(1)}, u32[]{:S(2)}, u32[]{:S(2)}) async-start(bf16[64,64,128]{2,0,1:T(8,128)(2,1)} %copy_bitcast_fusion), calls=%async_computation.2 | async-start | bytes 2097152 | tf_op jit(solution)/shard_map/all_to_all | solution.py:83
  204.0 0.3 all-reduce.4.cloned.1.call-start
  204.3 0.0 copy-start.21
  204.4 0.0 copy-done.5
  204.4 1.1 fusion.31
  205.5 0.5 copy-done.21
  206.0 4.0 fusion.33
  210.0 2.3 fusion.32
  212.3 20.6 %all-to-all-done.2 = bf16[64,64,128]{2,0,1:T(8,128)(2,1)S(1)} async-done(((bf16[64,64,128]{2,0,1:T(8,128)(2,1)}), bf16[64,64,128]{2,0,1:T(8,128)(2,1)S(1)}, u32[]{:S(2)}, u32[]{:S(2)}) %all-to-all-start.2) | async-done | bytes 1048608 | tf_op jit(solution)/shard_map/all_to_all | solution.py:83
  232.8 0.1 bitcast_bitcast_fusion
  233.0 2.8 copy.43
  235.8 44.6 %scatter_custom_fusion.1 = f32[64,2048]{0,1:T(8,128)S(1)} fusion(s32[8192]{0:T(1024)S(1)} %bitcast.124, f32[8192,64]{1,0:T(8,128)} %copy.43, f32[]{:T(128)} %constant.18.clone.1), kind=kCustom, calls=%fused_computation.48 | custom fusion | flops 524288 | bytes 524800 | tf_op jit(solution)/shard_map/scatter-add | solution.py:93
  280.4 0.3 copy.44
  280.7 0.2 multiply_convert_fusion.3
  280.9 0.0 copy-start.2
  280.9 2.8 fusion.13
  283.7 0.0 all-reduce.4.cloned.1.call-update
  283.8 1.4 fusion.27
  285.2 0.2 copy-done.3
  285.4 1.7 convolution_bitcast_fusion.1
  287.1 74.4 %all-reduce = (f32[16,64]{1,0:T(8,128)S(1)}, f32[64,64]{1,0:T(8,128)S(1)}) all-reduce(f32[16,64]{1,0:T(8,128)S(1)} %convolution_bitcast_fusion.1, f32[64,64]{1,0:T(8,128)S(1)} %fusion.27), channel_id=1, replica_groups=mesh['dp'=4,'graph'=64] {'dp','graph'}, use_global_device_ids=true, to_apply=%region_3.4 | all-reduce | flops 5120 | bytes 40960 | tf_op jit(solution)/shard_map/psum | solution.py:100
  361.5 0.6 broadcast_multiply_fusion.5
  362.1 0.6 broadcast_multiply_fusion.4
  362.7 4.3 fusion.4
  367.0 178.4 %all-reduce.4.cloned.1.call-done = (f32[512,64]{0,1:T(8,128)}, f32[64,512]{1,0:T(8,128)}, f32[512,512]{1,0:T(8,128)}, f32[512,512]{1,0:T(8,128)}) async-done(((f32[512,64]{0,1:T(8,128)}, f32[64,512]{1,0:T(8,128)}, f32[512,512]{1,0:T(8,128)}, f32[512,512]{1,0:T(8,128)}), (f32[512,64]{0,1:T(8,128)}, f32[64,512]{1,0:T(8,128)}, f32[512,512]{1,0:T(8,128)}, f32[512,512]{1,0:T(8,128)})) %all-reduce.4.cloned.1.call-update) | async-done | bytes 2359312 | tf_op jit(solution)/shard_map/psum | solution.py:100
  545.4 1.6 broadcast_multiply_fusion.3
  547.0 1.6 broadcast_multiply_fusion.2
  548.6 3.2 broadcast_multiply_fusion
  551.7 0.0 copy-done.1
  (38 shorter events, 0.2 us)
Async XLA Ops:
  7.2 140.7 %copy-start = (bf16[512,512]{1,0:T(8,128)(2,1)S(1)}, bf16[512,512]{1,0:T(8,128)(2,1)}, u32[]{:S(2)}) copy-start(bf16[512,512]{1,0:T(8,128)(2,1)} %param.22) | copy-start | bytes 1572868
  7.2 20.7 %all-to-all-start = ((s32[64,1,128]{2,1,0:T(1,128)}), s32[64,1,128]{2,1,0:T(1,128)S(1)}, u32[]{:S(2)}, u32[]{:S(2)}) async-start(s32[64,1,128]{2,1,0:T(1,128)} %bitcast.127), calls=%async_computation | async-start | bytes 65536 | tf_op jit(solution)/shard_map/all_to_all | solution.py:44
  53.6 9.2 %copy-start.8 = (s32[1,8192]{1,0:T(1,128)S(1)}, s32[1,8192]{1,0:T(1,128)}, u32[]{:S(2)}) copy-start(s32[1,8192]{1,0:T(1,128)} %param.17) | copy-start | bytes 98308
  53.6 9.3 %copy-start.9 = (bf16[1,16,8192]{2,1,0:T(8,128)(2,1)S(1)}, bf16[1,16,8192]{2,1,0:T(8,128)(2,1)}, u32[]{:S(2)}) copy-start(bf16[1,16,8192]{2,1,0:T(8,128)(2,1)} %param.15) | copy-start | bytes 786436
  53.6 9.3 %copy-start.13 = (bf16[16,64]{1,0:T(8,128)(2,1)S(1)}, bf16[16,64]{1,0:T(8,128)(2,1)}, u32[]{:S(2)}) copy-start(bf16[16,64]{1,0:T(8,128)(2,1)} %param.19) | copy-start | bytes 6148
  56.0 35.6 %all-to-all-start.1 = ((bf16[64,64,128]{2,0,1:T(8,128)(2,1)}), bf16[64,64,128]{2,0,1:T(8,128)(2,1)}, u32[]{:S(2)}, u32[]{:S(2)}) async-start(bf16[64,64,128]{2,0,1:T(8,128)(2,1)} %broadcast_select_fusion), calls=%async_computation.1 | async-start | bytes 2097152 | tf_op jit(solution)/shard_map/all_to_all | solution.py:51
  94.3 49.1 %copy-start.12 = (bf16[64,64]{1,0:T(8,128)(2,1)S(1)}, bf16[64,64]{1,0:T(8,128)(2,1)}, u32[]{:S(2)}) copy-start(bf16[64,64]{1,0:T(8,128)(2,1)} %param.20) | copy-start | bytes 24580
  98.1 46.9 %copy-start.11 = (bf16[64,512]{1,0:T(8,128)(2,1)S(1)}, bf16[64,512]{1,0:T(8,128)(2,1)}, u32[]{:S(2)}) copy-start(bf16[64,512]{1,0:T(8,128)(2,1)} %param.21) | copy-start | bytes 196612
  147.8 1.9 copy-start.16
  147.8 2.3 copy-start.14
  147.9 2.4 copy-start.15
  149.8 3.1 copy-start.20
  152.9 2.3 copy-start.22
  155.2 4.0 copy-start.18
  159.2 1.3 copy-start.4
  160.6 0.7 copy-start.6
  198.2 6.1 %copy-start.5 = (bf16[2048,512]{1,0:T(8,128)(2,1)S(1)}, bf16[2048,512]{1,0:T(8,128)(2,1)}, u32[]{:S(2)}) copy-start(bf16[2048,512]{1,0:T(8,128)(2,1)} %copy-done.4) | copy-start | bytes 6291460
  198.2 34.6 %all-to-all-start.2 = ((bf16[64,64,128]{2,0,1:T(8,128)(2,1)}), bf16[64,64,128]{2,0,1:T(8,128)(2,1)S(1)}, u32[]{:S(2)}, u32[]{:S(2)}) async-start(bf16[64,64,128]{2,0,1:T(8,128)(2,1)} %copy_bitcast_fusion), calls=%async_computation.2 | async-start | bytes 2097152 | tf_op jit(solution)/shard_map/all_to_all | solution.py:83
  204.0 341.4 %all-reduce.4.cloned.1.call-start = ((), (), s32[]{:S(2)}) async-start(), calls=%async_computation.3 | async-start | bytes 4718592 | tf_op jit(solution)/shard_map/psum | solution.py:100
  204.3 1.6 copy-start.21
  206.0 4.0 copy-start.17
  206.0 4.0 copy-start.19
  235.8 44.9 %copy-start.7 = (f32[64,2048]{1,0:T(8,128)S(1)}, f32[64,2048]{1,0:T(8,128)}, u32[]{:S(2)}) copy-start(f32[64,2048]{1,0:T(8,128)} %get-tuple-element.14) | copy-start | bytes 1572868
  280.9 2.9 copy-start.2
  283.7 1.7 copy-start.3
  285.4 77.3 %copy-start.10 = (bf16[512,64]{0,1:T(8,128)(2,1)S(1)}, bf16[512,64]{0,1:T(8,128)(2,1)}, u32[]{:S(2)}) copy-start(bf16[512,64]{0,1:T(8,128)(2,1)} %param.18) | copy-start | bytes 196612
  548.6 3.2 copy-start.1
Sparse Core Ops, SparseCore 0:
  283.9 261.4 all-reduce.3
where the time goes:
time: 560 us; the launch traced here: 559 us
  waiting for transfers between devices  231 us (41%)
  other arithmetic  107 us (19%)
  blocking collectives  74.4 us (13%)
  local copies, waits for them, and re-layouts  68.5 us (12%)
  matrix products  38.2 us (7%)
  starting transfers between devices  25.1 us (4%)
  between operations  15 us (3%)
    psum x1, waiting for transfers between devices, local(): lax.psum((down_grad, basis_grad, bilinear_grad, up_grad, first_grad, seco...  178 us
    psum x1, blocking collectives, local(): lax.psum((down_grad, basis_grad, bilinear_grad, up_grad, first_grad, seco...  74.4 us
    scatter-add x1, other arithmetic, local(): gathered = jnp.zeros((narrow, row_count), jnp.float32).at[:, out_local].a...  45.3 us
    scatter-add x1, other arithmetic, local(): jnp.zeros((narrow, row_count), jnp.float32).at[:, wanted].add(returned)  44.6 us
    dot_general x15, matrix products, contract(): lax.dot_general(left, right, (((left_dim,), (right_dim,)), ((), ())), pre...  33.7 us
    gather x2, local copies, waits for them, and re-layouts, local(): back_message = jnp.take(back_gathered, out_local, axis=1)  31.7 us
    all_to_all x1, waiting for transfers between devices, local(): lax.all_to_all(served, 'graph', split_axis=1, concat_axis=1, tiled=True)  28.1 us
    gather x2, local copies, waits for them, and re-layouts, local(): jnp.take(down_rows, wanted, axis=1).reshape(narrow, shards, slot_count)  25.6 us
  transfers between devices with their start and end apart: 4, of which 4 were waited for; matrix products, arithmetic and copies ran while one was open for 4% of the time, Pallas kernels for 0%

commit v1 on v0

--- a/solution.py
+++ b/solution.py
@@ -97,8 +97,12 @@
     back_pre = (back_down * silu_slope(pre_down)).astype(jnp.bfloat16)
     down_grad = contract(edge_rows, back_pre, 0, 1)
     edge_grad = (back_summed + contract(back_pre, down_weight, 0, 1)).astype(jnp.bfloat16)
-    down_grad, basis_grad, bilinear_grad, up_grad, first_grad, second_grad = lax.psum(
-        (down_grad, basis_grad, bilinear_grad, up_grad, first_grad, second_grad), ("dp", "graph")
+    down_grad, basis_grad, bilinear_grad, up_grad, first_grad, second_grad = jax.lax.psum(
+        jax.lax.psum(
+            (down_grad, basis_grad, bilinear_grad, up_grad, first_grad, second_grad),
+            axis_name="graph",
+        ),
+        axis_name="dp",
     )
     grad_scale = 1.0 / math.sqrt(lax.axis_size("dp") * shards * row_count)
     return (

time: 560 us -> 760 us (1.36)
  blocking collectives: 74.4 us -> 262 us
  waiting for transfers between devices: 231 us -> 240 us
    psum x1 -> x2, blocking collectives: 74.4 us -> 262 us  [the longest x1 245 us: local(): jax.lax.psum((down_grad, basis_grad, bilinear_grad, up_grad, first_grad,...]
    psum x1 -> x2, waiting for transfers between devices: 178 us -> 188 us  [the longest x1 188 us: local(): jax.lax.psum((down_grad, basis_grad, bilinear_grad, up_grad, first_grad,...]
  transfers between devices with their start and end apart: 4 -> 5, of which waited for: 4 -> 4; matrix products, arithmetic and copies ran while one was open for 4% -> 3% of each run, Pallas kernels for 0% -> 0%
where the time goes in v1:
time: 760 us; the launch traced here: 755 us
  blocking collectives  262 us (34%)
  waiting for transfers between devices  240 us (32%)
  other arithmetic  107 us (14%)
  local copies, waits for them, and re-layouts  68.3 us (9%)
  matrix products  37.9 us (5%)
  starting transfers between devices  25.1 us (3%)
  between operations  15.1 us (2%)
    psum x1, blocking collectives, local(): jax.lax.psum((down_grad, basis_grad, bilinear_grad, up_grad, first_grad,...  245 us
    psum x1, waiting for transfers between devices, local(): jax.lax.psum((down_grad, basis_grad, bilinear_grad, up_grad, first_grad,...  188 us
    scatter-add x1, other arithmetic, local(): gathered = jnp.zeros((narrow, row_count), jnp.float32).at[:, out_local].a...  45.3 us
    scatter-add x1, other arithmetic, local(): jnp.zeros((narrow, row_count), jnp.float32).at[:, wanted].add(returned)  44.6 us
    dot_general x15, matrix products, contract(): lax.dot_general(left, right, (((left_dim,), (right_dim,)), ((), ())), pre...  33.4 us
    gather x2, local copies, waits for them, and re-layouts, local(): back_message = jnp.take(back_gathered, out_local, axis=1)  31.7 us
    all_to_all x1, waiting for transfers between devices, local(): lax.all_to_all(served, 'graph', split_axis=1, concat_axis=1, tiled=True)  28.1 us
    gather x2, local copies, waits for them, and re-layouts, local(): jnp.take(down_rows, wanted, axis=1).reshape(narrow, shards, slot_count)  25.6 us
  transfers between devices with their start and end apart: 5, of which 4 were waited for; matrix products, arithmetic and copies ran while one was open for 3% of the time, Pallas kernels for 0%

profile of v1, /device:TPU:2, one launch (start us, length us, event | category | flops | bytes accessed | tf_op | source)
XLA Modules:
  0.0 755.3 jit_solution(9274414857364310888)
XLA Ops:
  7.2 0.0 copy-start
  7.2 12.2 %all-to-all-start = ((s32[64,1,128]{2,1,0:T(1,128)}), s32[64,1,128]{2,1,0:T(1,128)S(1)}, u32[]{:S(2)}, u32[]{:S(2)}) async-start(s32[64,1,128]{2,1,0:T(1,128)} %bitcast.127), calls=%async_computation | async-start | bytes 65536 | tf_op jit(solution)/shard_map/all_to_all | solution.py:44
  20.0 0.8 compare_and_fusion.1
  20.8 3.2 multiply_convert_fusion.4
  24.0 0.3 copy.35
  24.3 3.6 all-to-all-done
  28.0 24.0 %gather_fusion = bf16[8192,64]{1,0:T(8,128)(2,1)S(1)} fusion(bf16[64,2048]{0,1:T(8,128)(2,1)S(1)} %copy.35, s32[8192]{0:T(1024)S(1)} %broadcast_clamp_fusion.1), kind=kCustom, calls=%fused_computation | custom fusion | bytes 2129920 | tf_op jit(solution)/shard_map/jit(_take)/gather | solution.py:50
  52.0 1.6 copy.36
  53.6 2.4 broadcast_select_fusion
  56.0 6.9 all-to-all-start.1
  63.0 0.4 fusion.25
  63.4 28.1 %all-to-all-done.1 = bf16[64,64,128]{2,0,1:T(8,128)(2,1)} async-done(((bf16[64,64,128]{2,0,1:T(8,128)(2,1)}), bf16[64,64,128]{2,0,1:T(8,128)(2,1)}, u32[]{:S(2)}, u32[]{:S(2)}) %all-to-all-start.1) | async-done | bytes 1048608 | tf_op jit(solution)/shard_map/all_to_all | solution.py:51
  91.5 2.7 fusion.6
  94.3 3.8 copy.38
  98.1 45.3 %scatter_custom_fusion = f32[64,2048]{0,1:T(8,128)} fusion(s32[8192]{0:T(1024)S(1)} %bitcast.126, f32[8192,64]{1,0:T(8,128)} %copy.38, f32[]{:T(128)} %constant.18.clone.1), kind=kCustom, calls=%fused_computation.50 | custom fusion | flops 524288 | bytes 524800 | tf_op jit(solution)/shard_map/scatter-add | solution.py:58
  143.4 1.5 convolution_convert_fusion.1
  144.9 2.9 add_convert_fusion.1
  147.8 0.0 copy-start.14
  147.9 0.0 copy-start.15
  147.9 1.9 multiply_convert_fusion.2
  149.8 0.4 copy-done.14
  150.2 0.1 copy-done.15
  150.3 2.6 fusion.3
  152.9 2.3 multiply_convert_fusion.1
  155.3 4.0 multiply_convert_fusion
  159.2 0.7 convolution_convert_fusion
  160.0 0.6 copy-done.4
  160.6 0.7 copy-done.6
  161.3 1.0 convolution_bitcast_fusion
  162.3 1.4 copy.39
  163.6 27.9 %gather_fusion.1 = f32[8192,64]{1,0:T(8,128)} fusion(f32[64,2048]{0,1:T(8,128)S(1)} %copy.39, s32[8192]{0:T(1024)S(1)} %broadcast_clamp_fusion), kind=kCustom, calls=%fused_computation.1 | custom fusion | bytes 4227072 | tf_op jit(solution)/shard_map/jit(_take)/gather | solution.py:79
  191.6 3.8 copy.40
  195.3 2.9 copy_bitcast_fusion
  198.2 5.8 all-to-all-start.2
  204.0 0.3 all-reduce.7.cloned.1.call-start
  204.3 0.0 copy-done.5
  204.3 0.0 copy-start.21
  204.3 1.1 fusion.31
  205.5 0.5 copy-done.21
  206.0 4.0 fusion.33
  210.0 2.3 fusion.32
  212.3 20.6 %all-to-all-done.2 = bf16[64,64,128]{2,0,1:T(8,128)(2,1)S(1)} async-done(((bf16[64,64,128]{2,0,1:T(8,128)(2,1)}), bf16[64,64,128]{2,0,1:T(8,128)(2,1)S(1)}, u32[]{:S(2)}, u32[]{:S(2)}) %all-to-all-start.2) | async-done | bytes 1048608 | tf_op jit(solution)/shard_map/all_to_all | solution.py:83
  232.8 0.1 bitcast_bitcast_fusion
  233.0 2.8 copy.43
  235.8 44.6 %scatter_custom_fusion.1 = f32[64,2048]{0,1:T(8,128)S(1)} fusion(s32[8192]{0:T(1024)S(1)} %bitcast.124, f32[8192,64]{1,0:T(8,128)} %copy.43, f32[]{:T(128)} %constant.18.clone.1), kind=kCustom, calls=%fused_computation.48 | custom fusion | flops 524288 | bytes 524800 | tf_op jit(solution)/shard_map/scatter-add | solution.py:93
  280.4 0.3 copy.44
  280.7 0.2 multiply_convert_fusion.3
  280.9 2.7 fusion.13
  283.6 0.0 all-reduce.7.cloned.1.call-update
  283.7 0.0 copy-start.3
  283.7 0.0 all-reduce.9.cloned.1.call-start
  283.7 187.8 %all-reduce.7.cloned.1.call-done = (f32[512,64]{0,1:T(8,128)}, f32[64,512]{1,0:T(8,128)}, f32[512,512]{1,0:T(8,128)}, f32[512,512]{1,0:T(8,128)}) async-done(((f32[512,64]{0,1:T(8,128)}, f32[64,512]{1,0:T(8,128)}, f32[512,512]{1,0:T(8,128)}, f32[512,512]{1,0:T(8,128)}), (f32[512,64]{0,1:T(8,128)}, f32[64,512]{1,0:T(8,128)}, f32[512,512]{1,0:T(8,128)}, f32[512,512]{1,0:T(8,128)})) %all-reduce.7.cloned.1.call-update) | async-done | bytes 2359312 | tf_op jit(solution)/shard_map/psum | solution.py:101
  471.5 0.0 all-reduce.9.cloned.1.call-update
  471.6 1.2 fusion.27
  472.8 0.0 copy-start.10
  472.8 1.7 convolution_bitcast_fusion.1
  474.5 244.8 %all-reduce = (f32[16,64]{1,0:T(8,128)S(1)}, f32[64,64]{1,0:T(8,128)S(1)}) all-reduce(f32[16,64]{1,0:T(8,128)S(1)} %convolution_bitcast_fusion.1, f32[64,64]{1,0:T(8,128)S(1)} %fusion.27), channel_id=1, replica_groups=mesh['dp'=4,'graph'=64] {'graph'}, use_global_device_ids=true, to_apply=%region_4.5 | all-reduce | flops 5120 | bytes 40960 | tf_op jit(solution)/shard_map/psum | solution.py:101
  719.3 17.3 %all-reduce.2 = (f32[16,64]{1,0:T(8,128)S(1)}, f32[64,64]{1,0:T(8,128)S(1)}) all-reduce(f32[16,64]{1,0:T(8,128)S(1)} %get-tuple-element.7, f32[64,64]{1,0:T(8,128)S(1)} %get-tuple-element.8), channel_id=1, replica_groups=mesh['dp'=4,'graph'=64] {'dp'}, use_global_device_ids=true, to_apply=%region_5.6 | all-reduce | flops 5120 | bytes 40960 | tf_op jit(solution)/shard_map/psum | solution.py:100
  736.7 0.6 broadcast_multiply_fusion.5
  737.3 0.6 broadcast_multiply_fusion.4
  737.9 4.2 fusion.4
  742.2 1.6 broadcast_multiply_fusion.3
  743.7 1.6 broadcast_multiply_fusion.2
  745.3 3.2 broadcast_multiply_fusion
  (42 shorter events, 0.2 us)
Async XLA Ops:
  7.2 140.7 %copy-start = (bf16[512,512]{1,0:T(8,128)(2,1)S(1)}, bf16[512,512]{1,0:T(8,128)(2,1)}, u32[]{:S(2)}) copy-start(bf16[512,512]{1,0:T(8,128)(2,1)} %param.22) | copy-start | bytes 1572868
  7.2 20.7 %all-to-all-start = ((s32[64,1,128]{2,1,0:T(1,128)}), s32[64,1,128]{2,1,0:T(1,128)S(1)}, u32[]{:S(2)}, u32[]{:S(2)}) async-start(s32[64,1,128]{2,1,0:T(1,128)} %bitcast.127), calls=%async_computation | async-start | bytes 65536 | tf_op jit(solution)/shard_map/all_to_all | solution.py:44
  53.6 9.2 %copy-start.8 = (s32[1,8192]{1,0:T(1,128)S(1)}, s32[1,8192]{1,0:T(1,128)}, u32[]{:S(2)}) copy-start(s32[1,8192]{1,0:T(1,128)} %param.17) | copy-start | bytes 98308
  53.6 9.3 %copy-start.9 = (bf16[1,16,8192]{2,1,0:T(8,128)(2,1)S(1)}, bf16[1,16,8192]{2,1,0:T(8,128)(2,1)}, u32[]{:S(2)}) copy-start(bf16[1,16,8192]{2,1,0:T(8,128)(2,1)} %param.15) | copy-start | bytes 786436
  53.6 9.3 %copy-start.13 = (bf16[16,64]{1,0:T(8,128)(2,1)S(1)}, bf16[16,64]{1,0:T(8,128)(2,1)}, u32[]{:S(2)}) copy-start(bf16[16,64]{1,0:T(8,128)(2,1)} %param.19) | copy-start | bytes 6148
  56.0 35.6 %all-to-all-start.1 = ((bf16[64,64,128]{2,0,1:T(8,128)(2,1)}), bf16[64,64,128]{2,0,1:T(8,128)(2,1)}, u32[]{:S(2)}, u32[]{:S(2)}) async-start(bf16[64,64,128]{2,0,1:T(8,128)(2,1)} %broadcast_select_fusion), calls=%async_computation.1 | async-start | bytes 2097152 | tf_op jit(solution)/shard_map/all_to_all | solution.py:51
  94.3 49.1 %copy-start.12 = (bf16[64,64]{1,0:T(8,128)(2,1)S(1)}, bf16[64,64]{1,0:T(8,128)(2,1)}, u32[]{:S(2)}) copy-start(bf16[64,64]{1,0:T(8,128)(2,1)} %param.20) | copy-start | bytes 24580
  98.1 46.9 %copy-start.11 = (bf16[64,512]{1,0:T(8,128)(2,1)S(1)}, bf16[64,512]{1,0:T(8,128)(2,1)}, u32[]{:S(2)}) copy-start(bf16[64,512]{1,0:T(8,128)(2,1)} %param.21) | copy-start | bytes 196612
  147.8 1.9 copy-start.16
  147.8 2.3 copy-start.14
  147.9 2.4 copy-start.15
  149.8 3.1 copy-start.20
  152.9 2.3 copy-start.22
  155.2 4.0 copy-start.18
  159.2 1.3 copy-start.4
  160.6 0.7 copy-start.6
  198.2 6.1 copy-start.5
  198.2 34.6 %all-to-all-start.2 = ((bf16[64,64,128]{2,0,1:T(8,128)(2,1)}), bf16[64,64,128]{2,0,1:T(8,128)(2,1)S(1)}, u32[]{:S(2)}, u32[]{:S(2)}) async-start(bf16[64,64,128]{2,0,1:T(8,128)(2,1)} %copy_bitcast_fusion), calls=%async_computation.2 | async-start | bytes 2097152 | tf_op jit(solution)/shard_map/all_to_all | solution.py:83
  204.0 267.5 %all-reduce.7.cloned.1.call-start = ((), (), s32[]{:S(2)}) async-start(), calls=%async_computation.3 | async-start | bytes 4718592 | tf_op jit(solution)/shard_map/psum | solution.py:101
  204.3 1.6 copy-start.21
  206.0 4.0 copy-start.17
  206.0 4.0 copy-start.19
  235.8 44.9 %copy-start.7 = (f32[64,2048]{1,0:T(8,128)S(1)}, f32[64,2048]{1,0:T(8,128)}, u32[]{:S(2)}) copy-start(f32[64,2048]{1,0:T(8,128)} %get-tuple-element.20) | copy-start | bytes 1572868
  283.6 187.9 %copy-start.2 = (f32[64,2048]{0,1:T(8,128)S(1)}, f32[64,2048]{0,1:T(8,128)}, u32[]{:S(2)}) copy-start(f32[64,2048]{0,1:T(8,128)} %scatter_custom_fusion) | copy-start | bytes 1572868
  283.7 189.2 %copy-start.3 = (f32[8192,64]{0,1:T(8,128)S(1)}, f32[8192,64]{0,1:T(8,128)}, u32[]{:S(2)}) copy-start(f32[8192,64]{0,1:T(8,128)} %copy.40) | copy-start | bytes 6291460
  283.7 458.5 %all-reduce.9.cloned.1.call-start = ((), (), s32[]{:S(2)}) async-start(), calls=%async_computation.4 | async-start | bytes 4718592 | tf_op jit(solution)/shard_map/psum | solution.py:100
  472.8 265.1 %copy-start.10 = (bf16[512,64]{0,1:T(8,128)(2,1)S(1)}, bf16[512,64]{0,1:T(8,128)(2,1)}, u32[]{:S(2)}) copy-start(bf16[512,64]{0,1:T(8,128)(2,1)} %param.18) | copy-start | bytes 196612
  745.3 3.2 copy-start.1
Sparse Core Ops, SparseCore 0:
  283.8 187.6 all-reduce.6
  474.1 67.1 all-reduce.8
